TPU v7x, 32 devices: a whole 2x2x4 slice. The times are simulated.
32 devices in a mesh: ex: 4 (over y, x), ey: 2 (over core), tp: 4 (over z).
Axes of the slice: x: 2, y: 2, z: 4, core: 2. Of those that a mesh axis runs over, the one named last changes fastest.
Arguments:
- tokens: bfloat16 [256, 7168], P(('ex', 'ey'), 'tp'), may hold values from -6 to 6
- cotangent: bfloat16 [256, 7168], P(('ex', 'ey'), 'tp'), may hold values from -0.59765625 to 0.59765625
- gates: bfloat16 [256, 8], P(('ex', 'ey')), may hold values from 0.049804688 to 1
- expert_ids: int32 [256, 8], P(('ex', 'ey')), may hold values from 0 to 31, all different within a row; in each aligned block of 32 rows (0 to 31, 32 to 63, ...) at most 10 rows name the same one
- saved_gate: bfloat16 [1024, 32, 80], P(None, ('ex', 'ey')), may hold values from -6 to 6
- saved_up: bfloat16 [1024, 32, 80], P(None, ('ex', 'ey')), may hold values from -6 to 6
- w_gate: bfloat16 [32, 7168, 1024], P(('ex', 'ey'), 'tp'), may hold values from -0.1875 to 0.1875
- w_up: bfloat16 [32, 7168, 1024], P(('ex', 'ey'), 'tp'), may hold values from -0.1875 to 0.1875
- w_down: bfloat16 [32, 1024, 7168], P(('ex', 'ey'), None, 'tp'), may hold values from -0.25 to 0.25
Outputs:
- grad_tokens: bfloat16 [256, 7168], P(('ex', 'ey'), 'tp')
- grad_gates: bfloat16 [256, 8], P(('ex', 'ey'))
- grad_w_gate: bfloat16 [32, 7168, 1024], P(('ex', 'ey'), 'tp')
- grad_w_up: bfloat16 [32, 7168, 1024], P(('ex', 'ey'), 'tp')
- grad_w_down: bfloat16 [32, 1024, 7168], P(('ex', 'ey'), None, 'tp')
Inputs may be any that keep to these rules, and one draw needn't show every extreme that they name: `expert_ids`: each row names 8 different experts. The rows of one token group name any one expert at most 10 times, a bound that some block reaches.
All inputs are finite; a program needn't handle non-finite values.
Results may differ from a plain program's by a relative error of at most 0.025.
Values may be sent and summed in bfloat16 or wider, within the bound.
A program may use at most 128 MiB of HBM per device.

v0:
```python
import jax
import jax.numpy as jnp
from jax import lax
from jax.sharding import PartitionSpec as P

EXPERTS = 32
TOP = 8
CAP = 10


def slot_codes(expert_ids, capacity, expert_count):
    tok_rows, top_count = expert_ids.shape
    flat = expert_ids.reshape(-1)
    onehot = (flat[:, None] == jnp.arange(expert_count, dtype=jnp.int32)[None, :]).astype(jnp.int32)
    before = jnp.cumsum(onehot, axis=0) - onehot
    position = jnp.sum(before * onehot, axis=1)
    return (flat * capacity + position).reshape(tok_rows, top_count)


def pre_grads(dh_rows, gate_rows, up_rows):
    dh_wide = dh_rows.astype(jnp.float32)
    act_gate = gate_rows.astype(jnp.float32)
    act_up = up_rows.astype(jnp.float32)
    sigm = jax.nn.sigmoid(act_gate)
    d_gate_pre = (dh_wide * act_up * sigm * (1.0 + act_gate * (1.0 - sigm))).astype(jnp.bfloat16)
    d_up_pre = (dh_wide * act_gate * sigm).astype(jnp.bfloat16)
    return (d_gate_pre, d_up_pre)


def on_device(tokens, cotangent, gates, expert_ids, saved_gate, saved_up, w_gate, w_up, w_down):
    expert_count = EXPERTS
    capacity = CAP
    top_count = TOP
    local_width = tokens.shape[1]
    codes = slot_codes(expert_ids, capacity, expert_count)
    slot_rows = jnp.arange(expert_count * capacity, dtype=jnp.int32)
    tables = [
        (codes[:, k][None, :] == slot_rows[:, None]).astype(jnp.bfloat16) for k in range(top_count)
    ]
    chosen = tables[0]
    send_gate = jnp.dot(tables[0], gates[:, 0:1], preferred_element_type=jnp.float32)
    for k in range(1, top_count):
        chosen = chosen + tables[k]
        send_gate = send_gate + jnp.dot(
            tables[k], gates[:, k : k + 1], preferred_element_type=jnp.float32
        )
    send_x = jnp.dot(chosen, tokens, preferred_element_type=jnp.float32).astype(jnp.bfloat16)
    send_dy = jnp.dot(chosen, cotangent, preferred_element_type=jnp.float32).astype(jnp.bfloat16)
    send_x = send_x.reshape(expert_count, capacity, local_width)
    send_dy = send_dy.reshape(expert_count, capacity, local_width)
    send_gate = send_gate.astype(jnp.bfloat16).reshape(expert_count, capacity, 1)
    recv_x, recv_dy, recv_gate = (
        lax.all_to_all(send_x, ("ex", "ey"), split_axis=0, concat_axis=1, tiled=True),
        lax.all_to_all(send_dy, ("ex", "ey"), split_axis=0, concat_axis=1, tiled=True),
        lax.all_to_all(send_gate, ("ex", "ey"), split_axis=0, concat_axis=1, tiled=True),
    )
    scaled = (recv_gate.astype(jnp.float32) * recv_dy.astype(jnp.float32)).astype(jnp.bfloat16)
    gate_act = saved_gate.astype(jnp.float32)
    hidden = (gate_act * jax.nn.sigmoid(gate_act) * saved_up.astype(jnp.float32)).astype(
        jnp.bfloat16
    )
    out_rows = jnp.einsum("fes,efd->esd", hidden, w_down, preferred_element_type=jnp.float32)
    score_part = jnp.sum(recv_dy.astype(jnp.float32) * out_rows, axis=2).astype(jnp.bfloat16)
    dh_local = lax.psum_scatter(
        jnp.einsum("efd,esd->fes", w_down, scaled, preferred_element_type=jnp.float32).astype(
            jnp.bfloat16
        ),
        "tp",
        scatter_dimension=0,
        tiled=True,
    )
    dh_full, score_parts = (
        lax.all_gather(dh_local, "tp", axis=0, tiled=True),
        lax.all_gather(score_part[None], "tp", axis=0, tiled=True),
    )
    d_gate_pre, d_up_pre = pre_grads(dh_full, saved_gate, saved_up)
    score = jnp.sum(score_parts.astype(jnp.float32), axis=0).astype(jnp.bfloat16)
    dx_rows = jnp.einsum("fes,edf->esd", d_gate_pre, w_gate, preferred_element_type=jnp.float32)
    dx_rows = dx_rows + jnp.einsum(
        "fes,edf->esd", d_up_pre, w_up, preferred_element_type=jnp.float32
    )
    dx_rows = dx_rows.astype(jnp.bfloat16)
    grad_w_gate = jnp.einsum(
        "esd,fes->edf", recv_x, d_gate_pre, preferred_element_type=jnp.float32
    ).astype(jnp.bfloat16)
    grad_w_up = jnp.einsum(
        "esd,fes->edf", recv_x, d_up_pre, preferred_element_type=jnp.float32
    ).astype(jnp.bfloat16)
    grad_w_down = jnp.einsum(
        "fes,esd->efd", hidden, scaled, preferred_element_type=jnp.float32
    ).astype(jnp.bfloat16)
    score_col = score[:, :, None]
    back_dx, back_score = (
        lax.all_to_all(dx_rows, ("ex", "ey"), split_axis=1, concat_axis=0, tiled=True),
        lax.all_to_all(score_col, ("ex", "ey"), split_axis=1, concat_axis=0, tiled=True),
    )
    flat_dx = back_dx.reshape(expert_count * capacity, local_width)
    contract = (((0,), (0,)), ((), ()))
    grad_tokens = lax.dot_general(
        chosen, flat_dx, contract, preferred_element_type=jnp.float32
    ).astype(jnp.bfloat16)
    flat_score = back_score.reshape(expert_count * capacity, 1)
    columns = [
        lax.dot_general(tables[k], flat_score, contract, preferred_element_type=jnp.float32)
        for k in range(top_count)
    ]
    grad_gates = jnp.concatenate(columns, axis=1).astype(jnp.bfloat16)
    return (grad_tokens, grad_gates, grad_w_gate, grad_w_up, grad_w_down)


def solution(mesh):
    in_specs = (
        P(("ex", "ey"), "tp"),
        P(("ex", "ey"), "tp"),
        P(("ex", "ey"), None),
        P(("ex", "ey"), None),
        P(None, ("ex", "ey"), None),
        P(None, ("ex", "ey"), None),
        P(("ex", "ey"), "tp", None),
        P(("ex", "ey"), "tp", None),
        P(("ex", "ey"), None, "tp"),
    )
    out_specs = (
        P(("ex", "ey"), "tp"),
        P(("ex", "ey"), None),
        P(("ex", "ey"), "tp", None),
        P(("ex", "ey"), "tp", None),
        P(("ex", "ey"), None, "tp"),
    )
    return jax.shard_map(
        on_device, mesh=mesh, in_specs=in_specs, out_specs=out_specs, check_vma=False
    )
```

profile of v0, /device:TPU:0, one launch (start us, length us, event | category | flops | bytes accessed | tf_op | source)
XLA Modules:
  0.0 181.6 jit_solution(12350616389639696154)
XLA Ops:
  9.5 0.9 convolution_reduce_fusion
  10.4 0.9 convolution_reduce_fusion.1
  11.2 0.9 convolution_reduce_fusion.2
  12.1 0.9 convolution_reduce_fusion.3
  12.9 0.9 convolution_reduce_fusion.4
  13.8 0.9 convolution_reduce_fusion.5
  14.6 0.9 convolution_reduce_fusion.7
  15.5 0.9 convolution_reduce_fusion.6
  17.1 5.2 %all-to-all-start = ((bf16[32,10,1]{1,2,0:T(2,128)(2,1)}), bf16[32,10,1]{1,2,0:T(2,128)(2,1)S(1)}, u32[]{:S(2)}, u32[]{:S(2)}) async-start(bf16[32,10,1]{1,2,0:T(2,128)(2,1)} %reshape.205), calls=%async_computation | async-start | bytes 32768 | tf_op jit(solution)/shard_map/all_to_all | solution.py:55
  22.8 1.4 reshape.161
  24.2 2.8 %all-to-all-done = bf16[32,10,1]{1,2,0:T(2,128)(2,1)S(1)} async-done(((bf16[32,10,1]{1,2,0:T(2,128)(2,1)}), bf16[32,10,1]{1,2,0:T(2,128)(2,1)S(1)}, u32[]{:S(2)}, u32[]{:S(2)}) %all-to-all-start) | async-done | bytes 672 | tf_op jit(solution)/shard_map/all_to_all | solution.py:55
  27.0 3.6 %all-to-all-start.1 = ((bf16[32,10,1792]{2,1,0:T(8,128)(2,1)}), bf16[32,10,1792]{2,1,0:T(8,128)(2,1)S(1)}, u32[]{:S(2)}, u32[]{:S(2)}) async-start(bf16[32,10,1792]{2,1,0:T(8,128)(2,1)} %reshape.161), calls=%async_computation.1 | async-start | bytes 3670016 | tf_op jit(solution)/shard_map/all_to_all | solution.py:54
  31.2 1.4 reshape.164
  32.8 21.6 %all-to-all-done.1 = bf16[32,10,1792]{2,1,0:T(8,128)(2,1)S(1)} async-done(((bf16[32,10,1792]{2,1,0:T(8,128)(2,1)}), bf16[32,10,1792]{2,1,0:T(8,128)(2,1)S(1)}, u32[]{:S(2)}, u32[]{:S(2)}) %all-to-all-start.1) | async-done | bytes 1146912 | tf_op jit(solution)/shard_map/all_to_all | solution.py:54
  54.4 4.3 %all-to-all-start.4 = ((bf16[32,10,1792]{2,1,0:T(8,128)(2,1)}), bf16[32,10,1792]{2,1,0:T(8,128)(2,1)}, u32[]{:S(2)}, u32[]{:S(2)}) async-start(bf16[32,10,1792]{2,1,0:T(8,128)(2,1)} %reshape.164), calls=%async_computation.5 | async-start | bytes 3670016 | tf_op jit(solution)/shard_map/all_to_all | solution.py:53
  59.4 1.4 copy-done.3
  61.3 10.6 %fusion.12 = bf16[1024,4,80]{0,2,1:T(8,128)(2,1)} fusion(bf16[4,1024,1792]{2,1,0:T(8,128)(2,1)} %param.17, bf16[4,80,1792]{2,0,1:T(4,128)(2,1)S(1)} %multiply_convert_fusion), kind=kOutput, calls=%fused_computation.28 | convolution fusion | flops 1174732800 | bytes 16482304 | tf_op jit(solution)/shard_map/efd,esd->fes/dot_general | solution.py:65
  72.0 8.7 %fusion.1 = bf16[4,80]{1,0:T(4,128)(2,1)S(1)} fusion(bf16[4,1024,1792]{2,1,0:T(8,128)(2,1)} %param.17, f32[4,80,1792]{2,0,1:T(4,128)} %bitcast.140, bf16[1024,4,80]{0,2,1:T(8,128)(2,1)S(1)} %copy-done.4, bf16[1024,4,80]{0,2,1:T(8,128)(2,1)S(1)} %copy-done.2), kind=kOutput, calls=%fused_computation.16 | convolution fusion | flops 1178173184 | bytes 18285184 | tf_op jit(solution)/shard_map/fes,efd->esd/dot_general | solution.py:62
  80.7 11.3 %all-gather.1 = bf16[4,4,80]{2,1,0:T(4,128)(2,1)S(1)} all-gather(bf16[1,4,80]{2,1,0:T(4,128)(2,1)S(1)} %bitcast.145), channel_id=2, replica_groups=mesh['ex'=4,'ey'=2,'tp'=4] {'tp'}, dimensions={0}, use_global_device_ids=true | all-gather | bytes 3200 | tf_op jit(solution)/shard_map/all_gather | solution.py:74
  92.8 4.0 %all-to-all-start.3 = ((bf16[4,80,1]{0,2,1:T(2,128)(2,1)}), bf16[4,80,1]{0,2,1:T(2,128)(2,1)S(1)}, u32[]{:S(2)}, u32[]{:S(2)}) async-start(bf16[4,80,1]{0,2,1:T(2,128)(2,1)} %copy.77), calls=%async_computation.4 | async-start | bytes 81920 | tf_op jit(solution)/shard_map/all_to_all | solution.py:95
  96.7 7.6 %convolution_convert_fusion = bf16[4,1024,1792]{2,1,0:T(8,128)(2,1)} fusion(bf16[4,80,1792]{2,0,1:T(4,128)(2,1)S(1)} %multiply_convert_fusion, bf16[1024,4,80]{0,2,1:T(8,128)(2,1)S(1)} %copy-done.4, bf16[1024,4,80]{0,2,1:T(8,128)(2,1)S(1)} %copy-done.2), kind=kOutput, calls=%fused_computation | convolution fusion | flops 1184366592 | bytes 17137664 | tf_op jit(solution)/shard_map/fes,esd->efd/dot_general | solution.py:89
  104.3 2.1 %copy.80 = bf16[8,4,10,1792]{3,1,2,0:T(4,128)(2,1)S(1)} copy(bf16[8,4,10,1792]{3,2,1,0:T(8,128)(2,1)} %bitcast.37) | data formatting | bytes 2293760 | tf_op jit(solution)/shard_map/all_to_all | solution.py:53
  108.6 17.0 %all_gather.6 = bf16[1024,4,80]{0,2,1:T(8,128)(2,1)S(1)} all-gather(bf16[256,4,80]{0,2,1:T(8,128)(2,1)} %reduce-scatter.2.cloned.1.call-done), channel_id=1, replica_groups=mesh['ex'=4,'ey'=2,'tp'=4] {'tp'}, dimensions={0}, use_global_device_ids=true | all-gather | bytes 819200 | tf_op jit(solution)/shard_map/all_gather | solution.py:73
  125.6 11.1 %fusion.84 = f32[4,80,1792]{2,1,0:T(8,128)} fusion(bf16[4,1792,1024]{2,1,0:T(8,128)(2,1)} %param.15, bf16[1024,4,80]{0,2,1:T(8,128)(2,1)S(1)} %copy-done.4, bf16[1024,4,80]{0,2,1:T(8,128)(2,1)S(1)} %all_gather.6, bf16[1024,4,80]{0,2,1:T(8,128)(2,1)S(1)} %copy-done.2), kind=kOutput, calls=%fused_computation.133 | convolution fusion | flops 1178664960 | bytes 18939904 | tf_op jit(solution)/shard_map/fes,edf->esd/dot_general | solution.py:78
  136.8 11.4 %fusion = bf16[4,80,1792]{2,1,0:T(8,128)(2,1)} fusion(f32[4,80,1792]{2,1,0:T(8,128)} %fusion.84, bf16[4,1792,1024]{2,1,0:T(8,128)(2,1)} %param.16, bf16[1024,4,80]{0,2,1:T(8,128)(2,1)S(1)} %copy-done.2, bf16[1024,4,80]{0,2,1:T(8,128)(2,1)S(1)} %all_gather.6), kind=kOutput, calls=%fused_computation.5 | convolution fusion | flops 1178173440 | bytes 19431424 | tf_op jit(solution)/shard_map/fes,edf->esd/dot_general | solution.py:79
  148.1 2.9 %copy.74 = bf16[4,80,1792]{2,0,1:T(4,128)(2,1)} copy(bf16[4,80,1792]{2,1,0:T(8,128)(2,1)} %fusion) | data formatting | bytes 2293760 | tf_op jit(solution)/shard_map/convert_element_type | solution.py:82
  151.0 4.5 %all-to-all-start.2 = ((bf16[4,80,1792]{2,0,1:T(4,128)(2,1)}), bf16[4,80,1792]{2,0,1:T(4,128)(2,1)}, u32[]{:S(2)}, u32[]{:S(2)}) async-start(bf16[4,80,1792]{2,0,1:T(4,128)(2,1)} %copy.74), calls=%async_computation.3 | async-start | bytes 2293760 | tf_op jit(solution)/shard_map/all_to_all | solution.py:94
  155.5 7.6 %convolution_convert_fusion.2 = bf16[4,1792,1024]{2,1,0:T(8,128)(2,1)} fusion(bf16[4,80,1792]{2,0,1:T(4,128)(2,1)S(1)} %bitcast.138, bf16[1024,4,80]{0,2,1:T(8,128)(2,1)S(1)} %copy-done.4, bf16[1024,4,80]{0,2,1:T(8,128)(2,1)S(1)} %all_gather.6, bf16[1024,4,80]{0,2,1:T(8,128)(2,1)S(1)} %copy-done.2), kind=kOutput, calls=%fused_computation.2 | convolution fusion | flops 1186004992 | bytes 17793024 | tf_op jit(solution)/shard_map/esd,fes->edf/dot_general | solution.py:83
  163.1 7.6 %convolution_convert_fusion.1 = bf16[4,1792,1024]{2,1,0:T(8,128)(2,1)} fusion(bf16[4,80,1792]{2,0,1:T(4,128)(2,1)S(1)} %bitcast.139, bf16[1024,4,80]{0,2,1:T(8,128)(2,1)S(1)} %copy-done.2, bf16[1024,4,80]{0,2,1:T(8,128)(2,1)S(1)} %all_gather.6), kind=kOutput, calls=%fused_computation.1 | convolution fusion | flops 1184366592 | bytes 17137664 | tf_op jit(solution)/shard_map/esd,fes->edf/dot_general | solution.py:86
  170.7 1.0 all-to-all-done.2
  171.7 1.5 copy.75
  173.7 1.1 convolution_convert_fusion.5
  (55 shorter events, 8.9 us)
Async XLA Ops:
  7.2 15.1 %copy-start = (bf16[32,1792]{1,0:T(8,128)(2,1)S(1)}, bf16[32,1792]{1,0:T(8,128)(2,1)}, u32[]{:S(2)}) copy-start(bf16[32,1792]{1,0:T(8,128)(2,1)} %param.10) | copy-start | bytes 344068
  17.1 10.0 %all-to-all-start = ((bf16[32,10,1]{1,2,0:T(2,128)(2,1)}), bf16[32,10,1]{1,2,0:T(2,128)(2,1)S(1)}, u32[]{:S(2)}, u32[]{:S(2)}) async-start(bf16[32,10,1]{1,2,0:T(2,128)(2,1)} %reshape.205), calls=%async_computation | async-start | bytes 32768 | tf_op jit(solution)/shard_map/all_to_all | solution.py:55
  24.2 6.4 %copy-start.5 = (bf16[32,1792]{1,0:T(8,128)(2,1)S(1)}, bf16[32,1792]{1,0:T(8,128)(2,1)}, u32[]{:S(2)}) copy-start(bf16[32,1792]{1,0:T(8,128)(2,1)} %param.9) | copy-start | bytes 344068
  27.0 27.3 %all-to-all-start.1 = ((bf16[32,10,1792]{2,1,0:T(8,128)(2,1)}), bf16[32,10,1792]{2,1,0:T(8,128)(2,1)S(1)}, u32[]{:S(2)}, u32[]{:S(2)}) async-start(bf16[32,10,1792]{2,1,0:T(8,128)(2,1)} %reshape.161), calls=%async_computation.1 | async-start | bytes 3670016 | tf_op jit(solution)/shard_map/all_to_all | solution.py:54
  54.4 38.4 %all-to-all-start.4 = ((bf16[32,10,1792]{2,1,0:T(8,128)(2,1)}), bf16[32,10,1792]{2,1,0:T(8,128)(2,1)}, u32[]{:S(2)}, u32[]{:S(2)}) async-start(bf16[32,10,1792]{2,1,0:T(8,128)(2,1)} %reshape.164), calls=%async_computation.5 | async-start | bytes 3670016 | tf_op jit(solution)/shard_map/all_to_all | solution.py:53
  58.7 49.9 %reduce-scatter.2.cloned.1.call-start = ((), (), s32[]{:S(2)}) async-start(), calls=%async_computation.6 | async-start | bytes 819200 | tf_op jit(solution)/shard_map/reduce_scatter | solution.py:64
  59.3 1.4 copy-start.3
  61.3 10.7 %copy-start.2 = (bf16[1024,4,80]{0,2,1:T(8,128)(2,1)S(1)}, bf16[1024,4,80]{0,2,1:T(8,128)(2,1)}, u32[]{:S(2)}) copy-start(bf16[1024,4,80]{0,2,1:T(8,128)(2,1)} %param.13) | copy-start | bytes 1966084
  61.3 10.7 %copy-start.4 = (bf16[1024,4,80]{0,2,1:T(8,128)(2,1)S(1)}, bf16[1024,4,80]{0,2,1:T(8,128)(2,1)}, u32[]{:S(2)}) copy-start(bf16[1024,4,80]{0,2,1:T(8,128)(2,1)} %param.14) | copy-start | bytes 1966084
  92.8 13.7 %all-to-all-start.3 = ((bf16[4,80,1]{0,2,1:T(2,128)(2,1)}), bf16[4,80,1]{0,2,1:T(2,128)(2,1)S(1)}, u32[]{:S(2)}, u32[]{:S(2)}) async-start(bf16[4,80,1]{0,2,1:T(2,128)(2,1)} %copy.77), calls=%async_computation.4 | async-start | bytes 81920 | tf_op jit(solution)/shard_map/all_to_all | solution.py:95
  151.0 20.7 %all-to-all-start.2 = ((bf16[4,80,1792]{2,0,1:T(4,128)(2,1)}), bf16[4,80,1792]{2,0,1:T(4,128)(2,1)}, u32[]{:S(2)}, u32[]{:S(2)}) async-start(bf16[4,80,1792]{2,0,1:T(4,128)(2,1)} %copy.74), calls=%async_computation.3 | async-start | bytes 2293760 | tf_op jit(solution)/shard_map/all_to_all | solution.py:94
  173.2 1.5 copy-start.1
Sparse Core Ops, SparseCore 0:
  72.1 24.1 reduce-scatter.1
where the time goes:
time: 182 us
  matrix products  74.8 us (41%)
  blocking collectives  28.3 us (16%)
  waiting for transfers between devices  25.4 us (14%)
  starting transfers between devices  21.6 us (12%)
  local copies, waits for them, and re-layouts  15.9 us (9%)
  between operations  14.3 us (8%)
    all_to_all x1, waiting for transfers between devices, on_device(): lax.all_to_all(send_dy, ('ex', 'ey'), split_axis=0, concat_axis=1, tiled=...  21.6 us
    all_gather x1, blocking collectives, on_device(): lax.all_gather(dh_local, 'tp', axis=0, tiled=True)  17 us
    dot_general x1, matrix products, on_device(): jnp.einsum('fes,edf->esd', d_up_pre, w_up, preferred_element_type=jnp.flo...  11.4 us
    all_gather x1, blocking collectives, on_device(): lax.all_gather(score_part[None], 'tp', axis=0, tiled=True)  11.3 us
    dot_general x1, matrix products, on_device(): jnp.einsum('fes,edf->esd', d_gate_pre, w_gate, preferred_element_type=jnp...  11.1 us
    dot_general x1, matrix products, on_device(): jnp.einsum('efd,esd->fes', w_down, scaled, preferred_element_type=jnp.flo...  10.6 us
    dot_general x1, matrix products, on_device(): jnp.einsum('fes,efd->esd', hidden, w_down, preferred_element_type=jnp.flo...  8.72 us
    dot_general x1, matrix products, on_device(): jnp.einsum('esd,fes->edf', recv_x, d_gate_pre, preferred_element_type=jnp...  7.62 us
  transfers between devices with their start and end apart: 6, of which 3 were waited for; matrix products, arithmetic and copies ran while one was open for 29% of the time, Pallas kernels for 0%

commit v1 on v0

--- a/solution.py
+++ b/solution.py
@@ -6,6 +6,12 @@
 EXPERTS = 32
 TOP = 8
 CAP = 10
+
+
+def exchange_blocks(array, axis, split, join):
+    pieces = jnp.split(array, lax.axis_size(axis), axis=split)
+    arrived = lax.all_to_all(jnp.stack(pieces), axis, 0, 0)
+    return jnp.concatenate(arrived, axis=join)
 
 
 def slot_codes(expert_ids, capacity, expert_count):
@@ -51,7 +57,7 @@
     send_gate = send_gate.astype(jnp.bfloat16).reshape(expert_count, capacity, 1)
     recv_x, recv_dy, recv_gate = (
         lax.all_to_all(send_x, ("ex", "ey"), split_axis=0, concat_axis=1, tiled=True),
-        lax.all_to_all(send_dy, ("ex", "ey"), split_axis=0, concat_axis=1, tiled=True),
+        exchange_blocks(send_dy, ("ex", "ey"), 0, 1),
         lax.all_to_all(send_gate, ("ex", "ey"), split_axis=0, concat_axis=1, tiled=True),
     )
     scaled = (recv_gate.astype(jnp.float32) * recv_dy.astype(jnp.float32)).astype(jnp.bfloat16)

time: 182 us -> 175 us (0.962)
  waiting for transfers between devices: 25.4 us -> 14.5 us
  local copies, waits for them, and re-layouts: 15.9 us -> 19 us
    all_to_all x1, waiting for transfers between devices: 21.6 us -> 13.5 us  [exchange_blocks(): arrived = lax.all_to_all(jnp.stack(pieces), axis, 0, 0)]
    another operation x2 -> x12, local copies, waits for them, and re-layouts: 0.12 us -> 3.07 us  [the longest x10 2.94 us: exchange_blocks(): arrived = lax.all_to_all(jnp.stack(pieces), axis, 0, 0)]
    all_to_all x1, waiting for transfers between devices: 2.8 us -> 0.01 us  [on_device(): lax.all_to_all(send_gate, ('ex', 'ey'), split_axis=0, concat_axis=1, tile...]
  transfers between devices with their start and end apart: 6 -> 6, of which waited for: 3 -> 2; matrix products, arithmetic and copies ran while one was open for 29% -> 31% of each run, Pallas kernels for 0% -> 0%
where the time goes in v1:
time: 175 us; the launch traced here: 174 us
  matrix products  74.1 us (42%)
  blocking collectives  28.4 us (16%)
  starting transfers between devices  22.4 us (13%)
  local copies, waits for them, and re-layouts  19 us (11%)
  between operations  14.6 us (8%)
  waiting for transfers between devices  14.5 us (8%)
    all_gather x1, blocking collectives, on_device(): lax.all_gather(dh_local, 'tp', axis=0, tiled=True)  17.1 us
    all_to_all x1, waiting for transfers between devices, exchange_blocks(): arrived = lax.all_to_all(jnp.stack(pieces), axis, 0, 0)  13.5 us
    dot_general x1, matrix products, on_device(): jnp.einsum('fes,edf->esd', d_up_pre, w_up, preferred_element_type=jnp.flo...  11.4 us
    all_gather x1, blocking collectives, on_device(): lax.all_gather(score_part[None], 'tp', axis=0, tiled=True)  11.3 us
    dot_general x1, matrix products, on_device(): jnp.einsum('fes,edf->esd', d_gate_pre, w_gate, preferred_element_type=jnp...  11.1 us
    dot_general x1, matrix products, on_device(): jnp.einsum('efd,esd->fes', w_down, scaled, preferred_element_type=jnp.flo...  10.5 us
    dot_general x1, matrix products, on_device(): jnp.einsum('fes,efd->esd', hidden, w_down, preferred_element_type=jnp.flo...  8.15 us
    dot_general x1, matrix products, on_device(): jnp.einsum('fes,esd->efd', hidden, scaled, preferred_element_type=jnp.flo...  7.62 us
  transfers between devices with their start and end apart: 6, of which 2 were waited for; matrix products, arithmetic and copies ran while one was open for 31% of the time, Pallas kernels for 0%

profile of v1, /device:TPU:0, one launch (start us, length us, event | category | flops | bytes accessed | tf_op | source)
XLA Modules:
  0.0 174.4 jit_solution(9004810564996971288)
XLA Ops:
  9.6 0.9 convolution_reduce_fusion
  10.5 0.9 convolution_reduce_fusion.1
  11.3 0.9 convolution_reduce_fusion.2
  12.2 0.9 convolution_reduce_fusion.3
  13.0 0.9 convolution_reduce_fusion.4
  13.9 0.9 convolution_reduce_fusion.5
  14.7 0.9 convolution_reduce_fusion.7
  15.6 0.9 convolution_reduce_fusion.6
  17.2 5.2 %all-to-all-start = ((bf16[32,10,1]{1,2,0:T(2,128)(2,1)}), bf16[32,10,1]{1,2,0:T(2,128)(2,1)}, u32[]{:S(2)}, u32[]{:S(2)}) async-start(bf16[32,10,1]{1,2,0:T(2,128)(2,1)} %reshape.217), calls=%async_computation | async-start | bytes 32768 | tf_op jit(solution)/shard_map/all_to_all | solution.py:61
  24.9 1.0 stack.34
  26.0 1.6 copy.72
  27.7 4.3 %all-to-all-start.1 = ((bf16[8,4,10,1792]{3,1,2,0:T(4,128)(2,1)}), bf16[8,4,10,1792]{3,1,2,0:T(4,128)(2,1)S(1)}, u32[]{:S(2)}, u32[]{:S(2)}) async-start(bf16[8,4,10,1792]{3,1,2,0:T(4,128)(2,1)} %copy.72), calls=%async_computation.1 | async-start | bytes 2293760 | tf_op jit(solution)/shard_map/all_to_all | solution.py:13
  32.6 1.4 reshape.177
  35.0 13.5 %all-to-all-done.1 = bf16[8,4,10,1792]{3,1,2,0:T(4,128)(2,1)S(1)} async-done(((bf16[8,4,10,1792]{3,1,2,0:T(4,128)(2,1)}), bf16[8,4,10,1792]{3,1,2,0:T(4,128)(2,1)S(1)}, u32[]{:S(2)}, u32[]{:S(2)}) %all-to-all-start.1) | async-done | bytes 1146912 | tf_op jit(solution)/shard_map/all_to_all | solution.py:13
  48.4 4.3 %all-to-all-start.4 = ((bf16[32,10,1792]{2,1,0:T(8,128)(2,1)}), bf16[32,10,1792]{2,1,0:T(8,128)(2,1)}, u32[]{:S(2)}, u32[]{:S(2)}) async-start(bf16[32,10,1792]{2,1,0:T(8,128)(2,1)} %reshape.177), calls=%async_computation.5 | async-start | bytes 3670016 | tf_op jit(solution)/shard_map/all_to_all | solution.py:59
  53.3 10.5 %fusion.12 = bf16[1024,4,80]{0,2,1:T(8,128)(2,1)} fusion(bf16[4,1024,1792]{2,1,0:T(8,128)(2,1)} %param.17, bf16[4,80,1792]{2,0,1:T(4,128)(2,1)S(1)} %multiply_convert_fusion), kind=kOutput, calls=%fused_computation.28 | convolution fusion | flops 1174732800 | bytes 16482304 | tf_op jit(solution)/shard_map/efd,esd->fes/dot_general | solution.py:71
  64.1 0.9 copy-done.2
  65.2 8.2 %fusion.1 = bf16[4,80]{1,0:T(4,128)(2,1)S(1)} fusion(bf16[4,1024,1792]{2,1,0:T(8,128)(2,1)} %param.17, f32[4,80,1792]{2,0,1:T(4,128)S(1)} %bitcast.138, bf16[1024,4,80]{0,2,1:T(8,128)(2,1)S(1)} %copy-done.3, bf16[1024,4,80]{0,2,1:T(8,128)(2,1)S(1)} %copy-done.2), kind=kOutput, calls=%fused_computation.16 | convolution fusion | flops 1178173184 | bytes 18285184 | tf_op jit(solution)/shard_map/fes,efd->esd/dot_general | solution.py:68
  73.3 11.3 %all-gather.1 = bf16[4,4,80]{2,1,0:T(4,128)(2,1)S(1)} all-gather(bf16[1,4,80]{2,1,0:T(4,128)(2,1)S(1)} %bitcast.142), channel_id=2, replica_groups=mesh['ex'=4,'ey'=2,'tp'=4] {'tp'}, dimensions={0}, use_global_device_ids=true | all-gather | bytes 3200 | tf_op jit(solution)/shard_map/all_gather | solution.py:80
  85.4 4.0 %all-to-all-start.3 = ((bf16[4,80,1]{0,2,1:T(2,128)(2,1)}), bf16[4,80,1]{0,2,1:T(2,128)(2,1)S(1)}, u32[]{:S(2)}, u32[]{:S(2)}) async-start(bf16[4,80,1]{0,2,1:T(2,128)(2,1)} %copy.77), calls=%async_computation.4 | async-start | bytes 81920 | tf_op jit(solution)/shard_map/all_to_all | solution.py:101
  89.5 7.6 %convolution_convert_fusion = bf16[4,1024,1792]{2,1,0:T(8,128)(2,1)} fusion(bf16[4,80,1792]{2,0,1:T(4,128)(2,1)S(1)} %multiply_convert_fusion, bf16[1024,4,80]{0,2,1:T(8,128)(2,1)S(1)} %copy-done.4, bf16[1024,4,80]{0,2,1:T(8,128)(2,1)S(1)} %copy-done.2), kind=kOutput, calls=%fused_computation | convolution fusion | flops 1184366592 | bytes 17137664 | tf_op jit(solution)/shard_map/fes,esd->efd/dot_general | solution.py:95
  97.1 2.2 %copy.80 = bf16[8,4,10,1792]{3,1,2,0:T(4,128)(2,1)S(1)} copy(bf16[8,4,10,1792]{3,2,1,0:T(8,128)(2,1)} %bitcast.36) | data formatting | bytes 2293760 | tf_op jit(solution)/shard_map/all_to_all | solution.py:59
  101.4 17.1 %all_gather.6 = bf16[1024,4,80]{0,2,1:T(8,128)(2,1)S(1)} all-gather(bf16[256,4,80]{0,2,1:T(8,128)(2,1)} %reduce-scatter.2.cloned.1.call-done), channel_id=1, replica_groups=mesh['ex'=4,'ey'=2,'tp'=4] {'tp'}, dimensions={0}, use_global_device_ids=true | all-gather | bytes 819200 | tf_op jit(solution)/shard_map/all_gather | solution.py:79
  118.5 11.1 %fusion.84 = f32[4,80,1792]{2,1,0:T(8,128)} fusion(bf16[4,1792,1024]{2,1,0:T(8,128)(2,1)} %param.15, bf16[1024,4,80]{0,2,1:T(8,128)(2,1)S(1)} %copy-done.5, bf16[1024,4,80]{0,2,1:T(8,128)(2,1)S(1)} %all_gather.6, bf16[1024,4,80]{0,2,1:T(8,128)(2,1)S(1)} %copy-done.2), kind=kOutput, calls=%fused_computation.141 | convolution fusion | flops 1178664960 | bytes 18939904 | tf_op jit(solution)/shard_map/fes,edf->esd/dot_general | solution.py:84
  129.6 11.4 %fusion = bf16[4,80,1792]{2,1,0:T(8,128)(2,1)} fusion(f32[4,80,1792]{2,1,0:T(8,128)} %fusion.84, bf16[4,1792,1024]{2,1,0:T(8,128)(2,1)} %param.16, bf16[1024,4,80]{0,2,1:T(8,128)(2,1)S(1)} %copy-done.2, bf16[1024,4,80]{0,2,1:T(8,128)(2,1)S(1)} %all_gather.6), kind=kOutput, calls=%fused_computation.5 | convolution fusion | flops 1178173440 | bytes 19431424 | tf_op jit(solution)/shard_map/fes,edf->esd/dot_general | solution.py:85
  141.0 2.9 %copy.74 = bf16[4,80,1792]{2,0,1:T(4,128)(2,1)} copy(bf16[4,80,1792]{2,1,0:T(8,128)(2,1)} %fusion) | data formatting | bytes 2293760 | tf_op jit(solution)/shard_map/convert_element_type | solution.py:88
  143.9 4.5 %all-to-all-start.2 = ((bf16[4,80,1792]{2,0,1:T(4,128)(2,1)}), bf16[4,80,1792]{2,0,1:T(4,128)(2,1)}, u32[]{:S(2)}, u32[]{:S(2)}) async-start(bf16[4,80,1792]{2,0,1:T(4,128)(2,1)} %copy.74), calls=%async_computation.3 | async-start | bytes 2293760 | tf_op jit(solution)/shard_map/all_to_all | solution.py:100
  148.3 7.6 %convolution_convert_fusion.2 = bf16[4,1792,1024]{2,1,0:T(8,128)(2,1)} fusion(bf16[4,80,1792]{2,0,1:T(4,128)(2,1)S(1)} %bitcast.136, bf16[1024,4,80]{0,2,1:T(8,128)(2,1)S(1)} %copy-done.5, bf16[1024,4,80]{0,2,1:T(8,128)(2,1)S(1)} %all_gather.6, bf16[1024,4,80]{0,2,1:T(8,128)(2,1)S(1)} %copy-done.2), kind=kOutput, calls=%fused_computation.2 | convolution fusion | flops 1186004992 | bytes 17793024 | tf_op jit(solution)/shard_map/esd,fes->edf/dot_general | solution.py:89
  156.0 7.6 %convolution_convert_fusion.1 = bf16[4,1792,1024]{2,1,0:T(8,128)(2,1)} fusion(bf16[4,80,1792]{2,0,1:T(4,128)(2,1)S(1)} %bitcast.137, bf16[1024,4,80]{0,2,1:T(8,128)(2,1)S(1)} %copy-done.2, bf16[1024,4,80]{0,2,1:T(8,128)(2,1)S(1)} %all_gather.6), kind=kOutput, calls=%fused_computation.1 | convolution fusion | flops 1184366592 | bytes 17137664 | tf_op jit(solution)/shard_map/esd,fes->edf/dot_general | solution.py:92
  163.5 1.0 all-to-all-done.2
  164.6 1.5 copy.75
  166.5 1.1 convolution_convert_fusion.5
  (108 shorter events, 11.3 us)
Async XLA Ops:
  7.2 15.3 %copy-start = (bf16[32,1792]{1,0:T(8,128)(2,1)S(1)}, bf16[32,1792]{1,0:T(8,128)(2,1)}, u32[]{:S(2)}) copy-start(bf16[32,1792]{1,0:T(8,128)(2,1)} %param.10) | copy-start | bytes 344068
  9.5 12.9 %copy-start.8 = (s32[32]{0:T(128)}, s32[32]{0:T(128)S(1)}, u32[]{:S(2)}) copy-start(s32[32]{0:T(128)S(1)} %get-tuple-element.5) | copy-start | bytes 388
  9.5 12.8 %copy-start.10 = (s32[32]{0:T(128)}, s32[32]{0:T(128)S(1)}, u32[]{:S(2)}) copy-start(s32[32]{0:T(128)S(1)} %get-tuple-element.6) | copy-start | bytes 388
  9.5 12.8 %copy-start.12 = (s32[32]{0:T(128)}, s32[32]{0:T(128)S(1)}, u32[]{:S(2)}) copy-start(s32[32]{0:T(128)S(1)} %get-tuple-element.7) | copy-start | bytes 388
  9.5 12.8 %copy-start.14 = (s32[32]{0:T(128)}, s32[32]{0:T(128)S(1)}, u32[]{:S(2)}) copy-start(s32[32]{0:T(128)S(1)} %get-tuple-element.8) | copy-start | bytes 388
  9.6 12.8 %copy-start.16 = (s32[32]{0:T(128)}, s32[32]{0:T(128)S(1)}, u32[]{:S(2)}) copy-start(s32[32]{0:T(128)S(1)} %get-tuple-element.9) | copy-start | bytes 388
  9.6 12.8 %copy-start.18 = (s32[32]{0:T(128)}, s32[32]{0:T(128)S(1)}, u32[]{:S(2)}) copy-start(s32[32]{0:T(128)S(1)} %get-tuple-element.10) | copy-start | bytes 388
  9.6 12.8 %copy-start.20 = (s32[32]{0:T(128)}, s32[32]{0:T(128)S(1)}, u32[]{:S(2)}) copy-start(s32[32]{0:T(128)S(1)} %get-tuple-element.11) | copy-start | bytes 388
  9.6 12.8 %copy-start.22 = (s32[32]{0:T(128)}, s32[32]{0:T(128)S(1)}, u32[]{:S(2)}) copy-start(s32[32]{0:T(128)S(1)} %get-tuple-element.12) | copy-start | bytes 388
  17.2 10.5 %all-to-all-start = ((bf16[32,10,1]{1,2,0:T(2,128)(2,1)}), bf16[32,10,1]{1,2,0:T(2,128)(2,1)}, u32[]{:S(2)}, u32[]{:S(2)}) async-start(bf16[32,10,1]{1,2,0:T(2,128)(2,1)} %reshape.217), calls=%async_computation | async-start | bytes 32768 | tf_op jit(solution)/shard_map/all_to_all | solution.py:61
  23.8 0.9 copy-start.6
  27.6 4.4 %copy-start.7 = (bf16[32,1792]{1,0:T(8,128)(2,1)S(1)}, bf16[32,1792]{1,0:T(8,128)(2,1)}, u32[]{:S(2)}) copy-start(bf16[32,1792]{1,0:T(8,128)(2,1)} %param.9) | copy-start | bytes 344068
  27.6 4.4 %copy-start.9 = (s32[32]{0:T(128)S(1)}, s32[32]{0:T(128)}, u32[]{:S(2)}) copy-start(s32[32]{0:T(128)} %copy-done.8) | copy-start | bytes 388
  27.6 4.4 %copy-start.11 = (s32[32]{0:T(128)S(1)}, s32[32]{0:T(128)}, u32[]{:S(2)}) copy-start(s32[32]{0:T(128)} %copy-done.10) | copy-start | bytes 388
  27.6 4.4 %copy-start.13 = (s32[32]{0:T(128)S(1)}, s32[32]{0:T(128)}, u32[]{:S(2)}) copy-start(s32[32]{0:T(128)} %copy-done.12) | copy-start | bytes 388
  27.6 4.4 %copy-start.15 = (s32[32]{0:T(128)S(1)}, s32[32]{0:T(128)}, u32[]{:S(2)}) copy-start(s32[32]{0:T(128)} %copy-done.14) | copy-start | bytes 388
  27.6 4.4 %copy-start.17 = (s32[32]{0:T(128)S(1)}, s32[32]{0:T(128)}, u32[]{:S(2)}) copy-start(s32[32]{0:T(128)} %copy-done.16) | copy-start | bytes 388
  27.6 4.4 %copy-start.19 = (s32[32]{0:T(128)S(1)}, s32[32]{0:T(128)}, u32[]{:S(2)}) copy-start(s32[32]{0:T(128)} %copy-done.18) | copy-start | bytes 388
  27.6 4.4 %copy-start.21 = (s32[32]{0:T(128)S(1)}, s32[32]{0:T(128)}, u32[]{:S(2)}) copy-start(s32[32]{0:T(128)} %copy-done.20) | copy-start | bytes 388
  27.7 4.4 %copy-start.23 = (s32[32]{0:T(128)S(1)}, s32[32]{0:T(128)}, u32[]{:S(2)}) copy-start(s32[32]{0:T(128)} %copy-done.22) | copy-start | bytes 388
  27.7 20.8 %all-to-all-start.1 = ((bf16[8,4,10,1792]{3,1,2,0:T(4,128)(2,1)}), bf16[8,4,10,1792]{3,1,2,0:T(4,128)(2,1)S(1)}, u32[]{:S(2)}, u32[]{:S(2)}) async-start(bf16[8,4,10,1792]{3,1,2,0:T(4,128)(2,1)} %copy.72), calls=%async_computation.1 | async-start | bytes 2293760 | tf_op jit(solution)/shard_map/all_to_all | solution.py:13
  48.4 37.0 %all-to-all-start.4 = ((bf16[32,10,1792]{2,1,0:T(8,128)(2,1)}), bf16[32,10,1792]{2,1,0:T(8,128)(2,1)}, u32[]{:S(2)}, u32[]{:S(2)}) async-start(bf16[32,10,1792]{2,1,0:T(8,128)(2,1)} %reshape.177), calls=%async_computation.5 | async-start | bytes 3670016 | tf_op jit(solution)/shard_map/all_to_all | solution.py:59
  52.8 48.6 %reduce-scatter.2.cloned.1.call-start = ((), (), s32[]{:S(2)}) async-start(), calls=%async_computation.6 | async-start | bytes 819200 | tf_op jit(solution)/shard_map/reduce_scatter | solution.py:70
  63.9 1.1 copy-start.2
  63.9 1.3 copy-start.3
  65.2 24.3 %copy-start.4 = (bf16[1024,4,80]{0,2,1:T(8,128)(2,1)S(1)}, bf16[1024,4,80]{0,2,1:T(8,128)(2,1)}, u32[]{:S(2)}) copy-start(bf16[1024,4,80]{0,2,1:T(8,128)(2,1)} %param.14) | copy-start | bytes 1966084
  85.4 13.8 %all-to-all-start.3 = ((bf16[4,80,1]{0,2,1:T(2,128)(2,1)}), bf16[4,80,1]{0,2,1:T(2,128)(2,1)S(1)}, u32[]{:S(2)}, u32[]{:S(2)}) async-start(bf16[4,80,1]{0,2,1:T(2,128)(2,1)} %copy.77), calls=%async_computation.4 | async-start | bytes 81920 | tf_op jit(solution)/shard_map/all_to_all | solution.py:101
  97.1 21.4 %copy-start.5 = (bf16[1024,4,80]{0,2,1:T(8,128)(2,1)S(1)}, bf16[1024,4,80]{0,2,1:T(8,128)(2,1)}, u32[]{:S(2)}) copy-start(bf16[1024,4,80]{0,2,1:T(8,128)(2,1)} %param.14) | copy-start | bytes 1966084
  143.9 20.7 %all-to-all-start.2 = ((bf16[4,80,1792]{2,0,1:T(4,128)(2,1)}), bf16[4,80,1792]{2,0,1:T(4,128)(2,1)}, u32[]{:S(2)}, u32[]{:S(2)}) async-start(bf16[4,80,1792]{2,0,1:T(4,128)(2,1)} %copy.74), calls=%async_computation.3 | async-start | bytes 2293760 | tf_op jit(solution)/shard_map/all_to_all | solution.py:100
  166.1 1.5 copy-start.1
Sparse Core Ops, SparseCore 0:
  64.0 24.3 reduce-scatter.1
